TPU v7x, 32 devices: a whole 2x2x4 slice. The times are simulated.
32 devices in a mesh: groups: 2 (over y), seq: 4 (over z), mp: 4 (over x, core).
Axes of the slice: x: 2, y: 2, z: 4, core: 2. Of those that a mesh axis runs over, the one named last changes fastest.
Arguments:
- node_vectors: bfloat16 [1024, 2048], P(('groups', 'seq'), 'mp'), parts along dimension 0, may hold values from -6 to 6
- standardize_multiplier: float32 [2048], replicated, may hold values from 0.1 to 1.9
- probe_matrix: bfloat16 [2048, 1024], P(None, 'mp'), may hold values from -1 to 1
- lookup_matrix: bfloat16 [2048, 1024], P(None, 'mp'), may hold values from -1 to 1
- content_matrix: bfloat16 [2048, 1024], P(None, 'mp'), may hold values from -0.125 to 0.125
- softness_per_group: float32 [8], P('mp'), may hold values from 0.5 to 12
- exit_matrix: bfloat16 [1024, 2048], P('mp'), may hold values from -0.1875 to 0.1875
Outputs:
- mixed: bfloat16 [1024, 2048], P(('groups', 'seq'), 'mp'), parts along dimension 0
There are 2 independent parts, one for each index of `groups`. A program takes and returns all parts, laid end to end along the dimension named above; an argument that names none is the same for every part. Nothing has to cross between parts.
All inputs are finite; a program needn't handle non-finite values.
Results may differ from a plain program's by a relative error of at most 0.011.
Values may be sent and summed in bfloat16 or wider, within the bound.
A program may use at most 64 MiB of HBM per device.

v0:
```python
import math
import jax
import jax.numpy as jnp
from jax import lax
from jax.sharding import PartitionSpec as P


def attend(state_in, blocks, query_heads, inverse_root_span, resident_groups, channel_span):
    running_max, running_sum, weighted = state_in
    key_block, value_block = blocks
    count = key_block.shape[0]
    key_heads = key_block.reshape(count, resident_groups, channel_span)
    value_heads = value_block.reshape(count, resident_groups, channel_span)
    scores = (
        jnp.einsum("rhd,nhd->hrn", query_heads, key_heads, preferred_element_type=jnp.float32)
        * inverse_root_span[:, None, None]
    )
    new_max = jnp.max(scores, axis=-1)
    rescale = jnp.exp(running_max - new_max)
    weights = jnp.exp(scores - new_max[:, :, None])
    running_sum = running_sum * rescale + jnp.sum(weights, axis=-1)
    update = jnp.einsum(
        "hrn,nhd->hrd",
        weights.astype(jnp.bfloat16),
        value_heads,
        preferred_element_type=jnp.float32,
    )
    weighted = weighted * rescale[:, :, None] + update
    return (new_max, running_sum, weighted)


def per_device(
    node_vectors,
    standardize_multiplier,
    probe_matrix,
    lookup_matrix,
    content_matrix,
    softness_per_group,
    exit_matrix,
):
    full_rows = lax.all_gather(node_vectors, "mp", axis=1, tiled=True)
    widened = full_rows.astype(jnp.float32)
    average = jnp.mean(widened, axis=-1, keepdims=True)
    centered = widened - average
    variance = jnp.mean(centered * centered, axis=-1, keepdims=True)
    normed = (centered * lax.rsqrt(variance + 1e-05) * standardize_multiplier).astype(jnp.bfloat16)
    queries = jnp.dot(normed, probe_matrix, preferred_element_type=jnp.float32).astype(jnp.bfloat16)
    key_rows = jnp.dot(normed, lookup_matrix, preferred_element_type=jnp.float32).astype(
        jnp.bfloat16
    )
    value_rows = jnp.dot(normed, content_matrix, preferred_element_type=jnp.float32).astype(
        jnp.bfloat16
    )
    resident_groups = softness_per_group.shape[0]
    head_cols = queries.shape[1]
    channel_span = head_cols // resident_groups
    token_count = queries.shape[0]
    query_heads = queries.reshape(token_count, resident_groups, channel_span)
    inverse_root_span = softness_per_group / math.sqrt(channel_span)
    initial = (
        jnp.full((resident_groups, token_count), -jnp.inf, jnp.float32),
        jnp.zeros((resident_groups, token_count), jnp.float32),
        jnp.zeros((resident_groups, token_count, channel_span), jnp.float32),
    )
    final = attend(
        initial,
        (
            lax.all_gather(key_rows, "seq", axis=0, tiled=True),
            lax.all_gather(value_rows, "seq", axis=0, tiled=True),
        ),
        query_heads,
        inverse_root_span,
        resident_groups,
        channel_span,
    )
    heads_out = (
        (final[2] / final[1][:, :, None])
        .transpose(1, 0, 2)
        .reshape(token_count, head_cols)
        .astype(jnp.bfloat16)
    )
    partial_sums = jnp.dot(heads_out, exit_matrix, preferred_element_type=jnp.float32)
    summed = lax.psum_scatter(
        partial_sums.astype(jnp.bfloat16), "mp", scatter_dimension=1, tiled=True
    ).astype(jnp.float32)
    return (node_vectors.astype(jnp.float32) + summed).astype(jnp.bfloat16)


def solution(mesh):
    return jax.shard_map(
        per_device,
        mesh=mesh,
        in_specs=(
            P(("groups", "seq"), "mp"),
            P(),
            P(None, "mp"),
            P(None, "mp"),
            P(None, "mp"),
            P("mp"),
            P("mp", None),
        ),
        out_specs=P(("groups", "seq"), "mp"),
        check_vma=False,
    )
```

profile of v0, /device:TPU:0, one launch (start us, length us, event | category | flops | bytes accessed | tf_op | source)
XLA Modules:
  0.0 81.6 jit_solution(14585379958456140718)
XLA Ops:
  6.5 0.0 copy-start
  6.5 0.0 copy-start.2
  6.5 0.0 reduce-scatter.2.cloned.1.call-start
  6.5 0.8 broadcast_multiply_fusion
  7.3 8.8 %all_gather.9 = bf16[128,2048]{1,0:T(8,128)(2,1)S(1)} all-gather(bf16[128,512]{1,0:T(8,128)(2,1)} %param.7), channel_id=1, replica_groups=mesh['groups'=2,'seq'=4,'mp'=4] {'mp'}, dimensions={1}, use_global_device_ids=true | all-gather | bytes 655360 | tf_op jit(solution)/shard_map/all_gather | solution.py:41
  16.2 0.2 convert_reduce_fusion
  16.4 0.0 copy-start.5
  16.4 0.3 fusion.6
  16.7 0.0 copy-done.2
  16.7 0.4 copy-done.5
  17.1 0.0 copy-start.3
  17.1 0.4 convolution_convert_fusion.2
  17.4 0.9 %copy-done.3 = bf16[2048,256]{1,0:T(8,128)(2,1)S(1)} copy-done((bf16[2048,256]{1,0:T(8,128)(2,1)S(1)}, bf16[2048,256]{1,0:T(8,128)(2,1)}, u32[]{:S(2)}) %copy-start.3) | copy-done | bytes 1048600
  18.3 0.0 copy-start.4
  18.3 0.4 convolution_convert_fusion.1
  18.6 0.9 %copy-done.4 = bf16[2048,256]{1,0:T(8,128)(2,1)S(1)} copy-done((bf16[2048,256]{1,0:T(8,128)(2,1)S(1)}, bf16[2048,256]{1,0:T(8,128)(2,1)}, u32[]{:S(2)}) %copy-start.4) | copy-done | bytes 1048600
  19.5 0.4 fusion.5
  19.9 14.1 %all_gather.11 = bf16[512,256]{1,0:T(8,128)(2,1)S(1)} all-gather(bf16[128,256]{1,0:T(8,128)(2,1)S(1)} %convolution_convert_fusion.1), channel_id=1, replica_groups=mesh['groups'=2,'seq'=4,'mp'=4] {'seq'}, dimensions={0}, use_global_device_ids=true | all-gather | bytes 327680 | tf_op jit(solution)/shard_map/all_gather | solution.py:69
  34.0 0.1 copy.11
  34.1 14.6 %all_gather.10 = bf16[512,256]{1,0:T(8,128)(2,1)S(1)} all-gather(bf16[128,256]{1,0:T(8,128)(2,1)S(1)} %convolution_convert_fusion.2), channel_id=1, replica_groups=mesh['groups'=2,'seq'=4,'mp'=4] {'seq'}, dimensions={0}, use_global_device_ids=true | all-gather | bytes 327680 | tf_op jit(solution)/shard_map/all_gather | solution.py:68
  48.7 0.3 fusion.20
  49.1 0.2 fusion.9
  49.3 0.3 fusion.4
  49.6 0.0 copy-done
  49.6 1.1 %convolution_convert_fusion = bf16[128,2048]{1,0:T(8,128)(2,1)} fusion(bf16[128,256]{0,1:T(8,128)(2,1)S(1)} %bitcast.39, bf16[256,2048]{1,0:T(8,128)(2,1)S(1)} %copy-done), kind=kOutput, calls=%fused_computation | convolution fusion | flops 134479872 | bytes 1638400 | tf_op jit(solution)/shard_map/dot_general | solution.py:82
  50.8 0.0 copy-start.1
  50.8 0.0 reduce-scatter.2.cloned.1.call-update
  50.8 22.4 %reduce-scatter.2.cloned.1.call-done = bf16[128,512]{1,0:T(8,128)(2,1)} async-done(((bf16[128,2048]{1,0:T(8,128)(2,1)}), bf16[128,512]{1,0:T(8,128)(2,1)}) %reduce-scatter.2.cloned.1.call-update) | async-done | bytes 131088 | tf_op jit(solution)/shard_map/reduce_scatter | solution.py:83
  73.2 0.0 copy-done.1
  73.2 1.6 %add_convert_fusion = bf16[128,512]{1,0:T(8,128)(2,1)} fusion(bf16[128,512]{1,0:T(8,128)(2,1)} %reduce-scatter.2.cloned.1.call-done, bf16[128,512]{1,0:T(8,128)(2,1)S(1)} %copy-done.1), kind=kLoop, calls=%fused_computation.22 | loop fusion | flops 262144 | bytes 393216 | tf_op jit(solution)/shard_map/convert_element_type | solution.py:86
  (4 shorter events, 0.0 us)
Async XLA Ops:
  6.5 43.1 %copy-start = (bf16[256,2048]{1,0:T(8,128)(2,1)S(1)}, bf16[256,2048]{1,0:T(8,128)(2,1)}, u32[]{:S(2)}) copy-start(bf16[256,2048]{1,0:T(8,128)(2,1)} %param.13) | copy-start | bytes 3145732
  6.5 10.1 %copy-start.2 = (bf16[2048,256]{1,0:T(8,128)(2,1)S(1)}, bf16[2048,256]{1,0:T(8,128)(2,1)}, u32[]{:S(2)}) copy-start(bf16[2048,256]{1,0:T(8,128)(2,1)} %param.10) | copy-start | bytes 3145732
  6.5 66.6 %reduce-scatter.2.cloned.1.call-start = ((), (), s32[]{:S(2)}) async-start(), calls=%async_computation.1 | async-start | bytes 655360 | tf_op jit(solution)/shard_map/reduce_scatter | solution.py:83
  16.4 0.7 copy-start.5
  17.1 1.2 %copy-start.3 = (bf16[2048,256]{1,0:T(8,128)(2,1)S(1)}, bf16[2048,256]{1,0:T(8,128)(2,1)}, u32[]{:S(2)}) copy-start(bf16[2048,256]{1,0:T(8,128)(2,1)} %param.11) | copy-start | bytes 3145732
  18.3 1.2 %copy-start.4 = (bf16[2048,256]{1,0:T(8,128)(2,1)S(1)}, bf16[2048,256]{1,0:T(8,128)(2,1)}, u32[]{:S(2)}) copy-start(bf16[2048,256]{1,0:T(8,128)(2,1)} %param.9) | copy-start | bytes 3145732
  50.8 22.4 %copy-start.1 = (bf16[128,512]{1,0:T(8,128)(2,1)S(1)}, bf16[128,512]{1,0:T(8,128)(2,1)}, u32[]{:S(2)}) copy-start(bf16[128,512]{1,0:T(8,128)(2,1)} %param.7) | copy-start | bytes 393220
Sparse Core Ops, SparseCore 0:
  50.9 22.2 reduce-scatter.1
where the time goes:
time: 81.9 us; the launch traced here: 81.6 us
  blocking collectives  37.6 us (46%)
  waiting for transfers between devices  22.4 us (27%)
  between operations  13.5 us (16%)
  other arithmetic  3.1 us (4%)
  matrix products  2.85 us (3%)
  local copies, waits for them, and re-layouts  2.25 us (3%)
    reduce_scatter x1, waiting for transfers between devices, per_device(): lax.psum_scatter(partial_sums.astype(jnp.bfloat16), 'mp', scatter_dimensi...  22.4 us
    all_gather x1, blocking collectives, per_device(): lax.all_gather(key_rows, 'seq', axis=0, tiled=True)  14.6 us
    all_gather x1, blocking collectives, per_device(): lax.all_gather(value_rows, 'seq', axis=0, tiled=True)  14.1 us
    all_gather x1, blocking collectives, per_device(): full_rows = lax.all_gather(node_vectors, 'mp', axis=1, tiled=True)  8.84 us
    unnamed x12, local copies, waits for them, and re-layouts  2.11 us
  transfers between devices with their start and end apart: 1, of which 1 were waited for; matrix products, arithmetic and copies ran while one was open for 0% of the time, Pallas kernels for 0%

commit v1 on v0

--- a/solution.py
+++ b/solution.py
@@ -66,7 +66,9 @@
         initial,
         (
             lax.all_gather(key_rows, "seq", axis=0, tiled=True),
-            lax.all_gather(value_rows, "seq", axis=0, tiled=True),
+            jnp.concatenate(
+                lax.all_to_all(jnp.stack([value_rows] * lax.axis_size("seq")), "seq", 0, 0), axis=0
+            ),
         ),
         query_heads,
         inverse_root_span,

time: 81.9 us -> 72.5 us (0.89)
  blocking collectives: 37.6 us -> 24.7 us
  starting transfers between devices: 0.01 us -> 5 us
  waiting for transfers between devices: 22.4 us -> 21.4 us
    all_gather x1 -> x0, blocking collectives: 14.1 us -> none  [per_device(): lax.all_gather(value_rows, 'seq', axis=0, tiled=True)]
    all_to_all x0 -> x1, starting transfers between devices: none -> 5 us  [per_device(): lax.all_to_all(jnp.stack([value_rows] * lax.axis_size('seq')), 'seq', 0, 0)]
    all_gather x1, blocking collectives: 14.6 us -> 15.8 us  [per_device(): lax.all_gather(key_rows, 'seq', axis=0, tiled=True)]
    reduce_scatter x1, waiting for transfers between devices: 22.4 us -> 21.4 us  [per_device(): lax.psum_scatter(partial_sums.astype(jnp.bfloat16), 'mp', scatter_dimensi...]
    unnamed x12 -> x14, local copies, waits for them, and re-layouts: 2.11 us -> 1.25 us
    another operation x0 -> x2, local copies, waits for them, and re-layouts: none -> 0.84 us  [the longest x1 0.73 us: per_device(): jnp.stack([value_rows] * lax.axis_size('seq'))]
  transfers between devices with their start and end apart: 1 -> 2, of which waited for: 1 -> 1; matrix products, arithmetic and copies ran while one was open for 0% -> 2% of each run, Pallas kernels for 0% -> 0%
where the time goes in v1:
time: 72.5 us; the launch traced here: 72.2 us
  blocking collectives  24.7 us (34%)
  waiting for transfers between devices  21.4 us (30%)
  between operations  13.5 us (19%)
  starting transfers between devices  5 us (7%)
  matrix products  2.86 us (4%)
  local copies, waits for them, and re-layouts  2.41 us (3%)
  other arithmetic  2.3 us (3%)
    reduce_scatter x1, waiting for transfers between devices, per_device(): lax.psum_scatter(partial_sums.astype(jnp.bfloat16), 'mp', scatter_dimensi...  21.4 us
    all_gather x1, blocking collectives, per_device(): lax.all_gather(key_rows, 'seq', axis=0, tiled=True)  15.8 us
    all_gather x1, blocking collectives, per_device(): full_rows = lax.all_gather(node_vectors, 'mp', axis=1, tiled=True)  8.97 us
    all_to_all x1, starting transfers between devices, per_device(): lax.all_to_all(jnp.stack([value_rows] * lax.axis_size('seq')), 'seq', 0, 0)  5 us
    convert_element_type x1, other arithmetic, per_device(): return (node_vectors.astype(jnp.float32) + summed).astype(jnp.bfloat16)  1.59 us
  transfers between devices with their start and end apart: 2, of which 1 were waited for; matrix products, arithmetic and copies ran while one was open for 2% of the time, Pallas kernels for 0%

profile of v1, /device:TPU:0, one launch (start us, length us, event | category | flops | bytes accessed | tf_op | source)
XLA Modules:
  0.0 72.2 jit_solution(7887713855276321991)
XLA Ops:
  6.5 0.0 copy-start
  6.5 0.0 copy-start.2
  6.5 9.0 %all_gather.6 = bf16[128,2048]{1,0:T(8,128)(2,1)S(1)} all-gather(bf16[128,512]{1,0:T(8,128)(2,1)} %param.7), channel_id=1, replica_groups=mesh['groups'=2,'seq'=4,'mp'=4] {'mp'}, dimensions={1}, use_global_device_ids=true | all-gather | bytes 655360 | tf_op jit(solution)/shard_map/all_gather | solution.py:41
  15.5 0.2 convert_reduce_fusion
  15.7 0.0 copy-start.5
  15.7 0.3 fusion.6
  16.0 0.0 copy-done.2
  16.0 0.4 copy-done.5
  16.4 0.0 copy-start.3
  16.4 0.4 convolution_convert_fusion.1
  16.8 0.1 copy.13
  16.9 0.7 %stack.2 = bf16[4,128,256]{1,2,0:T(8,128)(2,1)} broadcast(bf16[128,256]{0,1:T(8,128)(2,1)S(1)} %copy.13), dimensions={1,2} | broadcast | bytes 327680 | tf_op jit(solution)/shard_map/stack | solution.py:70
  17.6 0.0 copy-start.6
  17.6 5.0 %all-to-all-start = ((bf16[4,128,256]{1,2,0:T(8,128)(2,1)}), bf16[4,128,256]{1,2,0:T(8,128)(2,1)S(1)}, u32[]{:S(2)}, u32[]{:S(2)}) async-start(bf16[4,128,256]{1,2,0:T(8,128)(2,1)} %stack.2), calls=%async_computation | async-start | bytes 524288 | tf_op jit(solution)/shard_map/all_to_all | solution.py:70
  22.6 0.0 reduce-scatter.2.cloned.1.call-start
  22.6 0.0 copy-done.6
  22.6 0.0 copy-done.3
  22.6 0.0 copy-start.4
  22.6 0.4 convolution_convert_fusion.2
  23.0 0.8 %copy-done.4 = bf16[2048,256]{1,0:T(8,128)(2,1)S(1)} copy-done((bf16[2048,256]{1,0:T(8,128)(2,1)S(1)}, bf16[2048,256]{1,0:T(8,128)(2,1)}, u32[]{:S(2)}) %copy-start.4) | copy-done | bytes 1048600
  23.9 0.4 fusion.5
  24.2 15.8 %all_gather.7 = bf16[512,256]{1,0:T(8,128)(2,1)S(1)} all-gather(bf16[128,256]{1,0:T(8,128)(2,1)S(1)} %convolution_convert_fusion.2), channel_id=1, replica_groups=mesh['groups'=2,'seq'=4,'mp'=4] {'seq'}, dimensions={0}, use_global_device_ids=true | all-gather | bytes 327680 | tf_op jit(solution)/shard_map/all_gather | solution.py:68
  40.0 0.3 fusion.20
  40.3 0.2 fusion.9
  40.5 0.0 all-to-all-done
  40.6 0.2 copy.14
  40.8 0.1 reshape_reshape.3
  40.9 0.3 fusion.4
  41.2 0.0 copy-done
  41.2 1.1 %convolution_convert_fusion = bf16[128,2048]{1,0:T(8,128)(2,1)} fusion(bf16[128,256]{0,1:T(8,128)(2,1)S(1)} %bitcast.39, bf16[256,2048]{1,0:T(8,128)(2,1)S(1)} %copy-done), kind=kOutput, calls=%fused_computation | convolution fusion | flops 134479872 | bytes 1638400 | tf_op jit(solution)/shard_map/dot_general | solution.py:84
  42.3 0.0 copy-start.1
  42.3 0.0 reduce-scatter.2.cloned.1.call-update
  42.4 21.4 %reduce-scatter.2.cloned.1.call-done = bf16[128,512]{1,0:T(8,128)(2,1)} async-done(((bf16[128,2048]{1,0:T(8,128)(2,1)}), bf16[128,512]{1,0:T(8,128)(2,1)}) %reduce-scatter.2.cloned.1.call-update) | async-done | bytes 131088 | tf_op jit(solution)/shard_map/reduce_scatter | solution.py:85
  63.7 0.0 copy-done.1
  63.8 1.6 %add_convert_fusion = bf16[128,512]{1,0:T(8,128)(2,1)} fusion(bf16[128,512]{1,0:T(8,128)(2,1)} %reduce-scatter.2.cloned.1.call-done, bf16[128,512]{1,0:T(8,128)(2,1)S(1)} %copy-done.1), kind=kLoop, calls=%fused_computation.22 | loop fusion | flops 262144 | bytes 393216 | tf_op jit(solution)/shard_map/convert_element_type | solution.py:88
  (5 shorter events, 0.0 us)
Async XLA Ops:
  6.5 34.7 %copy-start = (bf16[256,2048]{1,0:T(8,128)(2,1)S(1)}, bf16[256,2048]{1,0:T(8,128)(2,1)}, u32[]{:S(2)}) copy-start(bf16[256,2048]{1,0:T(8,128)(2,1)} %param.13) | copy-start | bytes 3145732
  6.5 9.4 %copy-start.2 = (bf16[2048,256]{1,0:T(8,128)(2,1)S(1)}, bf16[2048,256]{1,0:T(8,128)(2,1)}, u32[]{:S(2)}) copy-start(bf16[2048,256]{1,0:T(8,128)(2,1)} %param.11) | copy-start | bytes 3145732
  15.7 0.7 copy-start.5
  16.4 6.2 %copy-start.3 = (bf16[2048,256]{1,0:T(8,128)(2,1)S(1)}, bf16[2048,256]{1,0:T(8,128)(2,1)}, u32[]{:S(2)}) copy-start(bf16[2048,256]{1,0:T(8,128)(2,1)} %param.10) | copy-start | bytes 3145732
  17.6 5.0 %copy-start.6 = (f32[2]{0:T(128)S(1)}, f32[2]{0:T(128)}, u32[]{:S(2)}) copy-start(f32[2]{0:T(128)} %param.12) | copy-start | bytes 28
  17.6 22.9 %all-to-all-start = ((bf16[4,128,256]{1,2,0:T(8,128)(2,1)}), bf16[4,128,256]{1,2,0:T(8,128)(2,1)S(1)}, u32[]{:S(2)}, u32[]{:S(2)}) async-start(bf16[4,128,256]{1,2,0:T(8,128)(2,1)} %stack.2), calls=%async_computation | async-start | bytes 524288 | tf_op jit(solution)/shard_map/all_to_all | solution.py:70
  22.6 41.1 %reduce-scatter.2.cloned.1.call-start = ((), (), s32[]{:S(2)}) async-start(), calls=%async_computation.2 | async-start | bytes 655360 | tf_op jit(solution)/shard_map/reduce_scatter | solution.py:85
  22.6 1.2 %copy-start.4 = (bf16[2048,256]{1,0:T(8,128)(2,1)S(1)}, bf16[2048,256]{1,0:T(8,128)(2,1)}, u32[]{:S(2)}) copy-start(bf16[2048,256]{1,0:T(8,128)(2,1)} %param.9) | copy-start | bytes 3145732
  42.3 21.4 %copy-start.1 = (bf16[128,512]{1,0:T(8,128)(2,1)S(1)}, bf16[128,512]{1,0:T(8,128)(2,1)}, u32[]{:S(2)}) copy-start(bf16[128,512]{1,0:T(8,128)(2,1)} %param.7) | copy-start | bytes 393220
Sparse Core Ops, SparseCore 0:
  42.5 21.2 reduce-scatter.1
